TPU v7x, 128 devices: a whole 4x4x4 slice. The times are simulated.
128 devices in a mesh: pair: 2 (over x_hi), gx: 8 (over y, x_lo), gy: 8 (over z, core).
Axes of the slice: x: 4 (x_hi: 2, x_lo: 2; x = x_hi * 2 + x_lo), y: 4, z: 4, core: 2. Of those that a mesh axis runs over, the one named last changes fastest.
Arguments:
- sound_speed_sq: float32 [64, 64, 1024], P('gx', 'gy'), may hold values from 0.5 to 2
- wind_profile: float32 [3, 1024], replicated, may hold values from -0.6 to 0.6
- forward_field: bfloat16 [4, 4, 64, 64, 1024], P(None, None, 'gx', 'gy'), may hold values from -6 to 6
- adjoint_state: float32 [2, 4, 64, 64, 1024], P('pair', None, 'gx', 'gy'), may hold values from -0.3125 to 0.3125
- pair_counts: int32 [2], P('pair'), may hold values from 64 to 256, as said below
- source_cells: int32 [512, 3], P('pair'), may hold values from 0 to 1023, as said below
- receiver_cells: int32 [512, 3], P('pair'), may hold values from 0 to 1023, as said below
- residuals: float32 [512, 4], P('pair'), may hold values from -16 to 16
Outputs:
- kernels: float32 [4, 64, 64, 1024], P(None, 'gx', 'gy', 'pair')
- final_state: float32 [2, 4, 64, 64, 1024], P('pair', None, 'gx', 'gy')
Inputs may be any that keep to these rules, and one draw needn't show every extreme that they name: `pair_counts`: one group in every draw has exactly 256 live pairs. `source_cells`: columns are the cell along the first, second and third dimension, each within the grid. `receiver_cells`: columns are the cell along the first, second and third dimension, each within the grid; several pairs may share a cell.
All inputs are finite; a program needn't handle non-finite values.
Results may differ from a plain program's by a relative error of at most 0.00115.
Values may be sent and summed in bfloat16 or wider, within the bound.
A program may use at most 128 MiB of HBM per device.

v0:
```python
import jax
import jax.numpy as jnp
from jax import lax
from jax.sharding import PartitionSpec as P

step_length = 0.25


def extended(shard, sides, width):
    for axis, dim in sides:
        size, length = (lax.axis_size(axis), shard.shape[dim])
        up = [(i, (i + 1) % size) for i in range(size - 1)]
        down = [(j, i) for i, j in up]
        last = lax.slice_in_dim(shard, length - width, length, axis=dim)
        initial = lax.slice_in_dim(shard, 0, width, axis=dim)
        before = lax.ppermute(last, axis, up)
        after = lax.ppermute(initial, axis, down)
        shard = jnp.concatenate([before, shard, after], axis=dim)
    return shard


def central(padded):
    dims = padded.ndim
    east_diff = (padded[..., 2:, 1:-1, :] - padded[..., :-2, 1:-1, :]) * 0.5
    north_diff = (padded[..., 1:-1, 2:, :] - padded[..., 1:-1, :-2, :]) * 0.5
    center = padded[..., 1:-1, 1:-1, :]
    vertical = jnp.pad(center, [(0, 0)] * (dims - 1) + [(1, 1)])
    up_diff = (vertical[..., 2:] - vertical[..., :-2]) * 0.5
    return (east_diff, north_diff, up_diff, center)


def local_flat(cells, width_x, width_y, depth):
    local_x = cells[:, 0] - lax.axis_index("gx") * width_x
    local_y = cells[:, 1] - lax.axis_index("gy") * width_y
    inside = (local_x >= 0) & (local_x < width_x) & (local_y >= 0) & (local_y < width_y)
    flat = (
        jnp.clip(local_x, 0, width_x - 1) * width_y + jnp.clip(local_y, 0, width_y - 1)
    ) * depth + cells[:, 2]
    return (flat, inside.astype(jnp.float32))


def shards(
    sound_speed_sq,
    wind_profile,
    forward_field,
    adjoint_state,
    pair_counts,
    source_cells,
    receiver_cells,
    residuals,
):
    steps_total = forward_field.shape[0]
    width_x, width_y, depth = sound_speed_sq.shape
    slots = residuals.shape[0]
    east_wind = wind_profile[0]
    north_wind = wind_profile[1]
    vertical_wind = wind_profile[2]
    live = (jnp.arange(slots, dtype=jnp.int32) < pair_counts[0]).astype(jnp.float32)
    src_flat, src_inside = local_flat(source_cells, width_x, width_y, depth)
    rcv_flat, rcv_inside = local_flat(receiver_cells, width_x, width_y, depth)
    pressure_snaps = forward_field[:, 0].reshape(steps_total, -1)
    local_samples = (
        jnp.take(pressure_snaps, src_flat, axis=1).astype(jnp.float32) * src_inside[None, :]
    )
    samples = lax.psum(local_samples, ("gx", "gy"))
    state = adjoint_state[0]
    kernel_local = jnp.zeros((4, width_x, width_y, depth), jnp.float32)
    for step in range(steps_total):
        snap = steps_total - 1 - step
        amplitude = residuals[:, snap] * samples[snap] * live * rcv_inside
        injected = (
            jnp.zeros((width_x * width_y * depth,), jnp.float32)
            .at[rcv_flat]
            .add(amplitude)
            .reshape(width_x, width_y, depth)
        )
        padded = extended(state, (("gx", 1), ("gy", 2)), 1)
        east_diff, north_diff, up_diff, center = central(padded)
        pressure = center[0]
        velocity = center[1:]
        divergence = east_diff[1] + north_diff[2] + up_diff[3]
        p_new = (
            pressure
            + step_length
            * (
                sound_speed_sq * divergence
                + east_wind * east_diff[0]
                + north_wind * north_diff[0]
                + vertical_wind * up_diff[0]
            )
            + injected
        )
        p_padded = extended(p_new, (("gx", 0), ("gy", 1)), 1)
        p_east, p_north, p_up, unused_center = central(p_padded)
        gradient = jnp.stack([p_east, p_north, p_up])
        a_new = velocity + step_length * (
            gradient
            + east_wind * east_diff[1:]
            + north_wind * north_diff[1:]
            + vertical_wind * up_diff[1:]
        )
        forward_rim = extended(forward_field[snap], (("gx", 1), ("gy", 2)), 1).astype(jnp.float32)
        f_east, f_north, f_up, unused_forward = central(forward_rim)
        pieces = [p_new * (f_east[1] + f_north[2] + f_up[3])]
        for along in (f_east, f_north, f_up):
            pieces.append(
                p_new * along[0] + a_new[0] * along[1] + a_new[1] * along[2] + a_new[2] * along[3]
            )
        increment = jnp.stack(pieces)
        kernel_local = kernel_local + increment
        state = jnp.concatenate([p_new[None], a_new], axis=0)
    kernels = lax.psum_scatter(kernel_local, "pair", scatter_dimension=3, tiled=True)
    return (kernels, state[None])


def solution(mesh):
    in_specs = (
        P("gx", "gy", None),
        P(),
        P(None, None, "gx", "gy", None),
        P("pair", None, "gx", "gy", None),
        P("pair"),
        P("pair", None),
        P("pair", None),
        P("pair", None),
    )
    out_specs = (P(None, "gx", "gy", "pair"), P("pair", None, "gx", "gy", None))
    return jax.shard_map(shards, mesh=mesh, in_specs=in_specs, out_specs=out_specs, check_vma=False)
```

profile of v0, /device:TPU:1, one launch (start us, length us, event | category | flops | bytes accessed | tf_op | source)
XLA Modules:
  0.0 556.1 jit_solution(320897750737244086)
XLA Ops:
  7.2 1.8 slice_bitcast_fusion
  11.0 5.2 collective-permute-start.4
  17.0 3.7 collective-permute-start.1
  20.6 1.3 collective-permute-start
  23.9 1.9 slice.831
  26.9 13.0 %copy.11 = bf16[4,1,8,8,1024]{0,4,3,2,1:T(8,128)(2,1)} copy(bf16[4,1,8,8,1024]{4,3,2,1,0:T(8,128)(2,1)} %slice.831) | data formatting | bytes 1048576 | tf_op jit(solution)/shard_map/slice | solution.py:61
  40.0 8.7 %gather_fusion = bf16[256,4]{1,0:T(8,128)(2,1)S(1)} fusion(bf16[4,65536]{0,1:T(8,128)(2,1)} %bitcast.532, s32[1024]{0:T(1024)S(1)} %pad_clamp_fusion), kind=kCustom, calls=%fused_computation | custom fusion | bytes 5120 | tf_op jit(solution)/shard_map/jit(_take)/gather | solution.py:63
  48.8 278.8 %psum.7 = f32[4,256]{0,1:T(8,128)S(1)} all-reduce(f32[4,256]{0,1:T(8,128)S(1)} %multiply_bitcast_fusion), channel_id=1, replica_groups=mesh['pair'=2,'gx'=8,'gy'=8] {'gx','gy'}, use_global_device_ids=true, to_apply=%region_0.1 | all-reduce | flops 1024 | bytes 8192 | tf_op jit(solution)/shard_map/psum | solution.py:65
  332.6 2.2 scatter_custom_fusion
  335.5 2.2 scatter_custom_fusion.1
  338.5 2.2 scatter_custom_fusion.2
  341.4 2.8 scatter_custom_fusion.3
  345.2 1.3 collective-permute-start.16
  349.0 4.0 collective-permute-start.28
  355.5 4.0 collective-permute-start.40
  359.5 9.9 %collective-permute-start.7 = (bf16[4,10,1,1024]{3,2,1,0:T(2,128)(2,1)S(1)}, bf16[4,10,1,1024]{3,2,1,0:T(2,128)(2,1)S(1)}, u32[]{:S(2)}, u32[]{:S(2)}) collective-permute-start(bf16[4,10,1,1024]{3,2,1,0:T(2,128)(2,1)S(1)} %get-tuple-element.75), channel_id=1, source_target_pairs={{1,0},{2,1},{3,2},{4,3},{5,4},{6,5},{7,6},{9,8},{10,9},{11,10},{12... | collective-permute-start | bytes 245768 | tf_op jit(solution)/shard_map/ppermute | solution.py:17
  369.6 1.9 collective-permute-start.6
  371.5 2.4 collective-permute-start.19
  374.2 3.2 collective-permute-start.18
  377.3 1.9 collective-permute-start.31
  380.5 3.6 collective-permute-start.3
  384.1 2.1 collective-permute-start.2
  386.2 1.6 maximum_convert_fusion
  389.1 3.8 collective-permute-start.30
  392.9 1.9 collective-permute-start.43
  394.8 1.9 fusion.39
  397.1 2.5 collective-permute-start.9
  400.9 1.5 maximum_convert_fusion.1
  402.5 1.8 collective-permute-done.8
  404.4 5.1 collective-permute-start.11
  409.4 1.9 collective-permute-start.10
  412.0 2.8 collective-permute-done.10
  415.5 2.5 collective-permute-start.13
  420.0 2.7 collective-permute-start.42
  423.9 3.3 collective-permute-start.15
  427.3 1.9 collective-permute-start.14
  429.9 4.0 collective-permute-done.14
  435.4 2.5 collective-permute-start.21
  439.9 2.7 collective-permute-done.20
  442.6 3.2 collective-permute-start.23
  445.8 1.9 collective-permute-start.22
  448.5 2.7 collective-permute-done.22
  451.9 2.5 collective-permute-start.25
  456.3 3.8 collective-permute-done.24
  460.3 3.3 collective-permute-start.27
  463.7 2.1 collective-permute-start.26
  467.1 3.2 collective-permute-done.26
  471.8 2.6 collective-permute-start.33
  476.0 3.0 collective-permute-done.32
  479.1 3.2 collective-permute-start.35
  482.3 1.9 collective-permute-start.34
  484.4 3.2 collective-permute-done.34
  488.3 2.5 collective-permute-start.37
  492.8 3.8 collective-permute-done.36
  496.8 4.3 collective-permute-start.39
  501.1 1.9 collective-permute-start.38
  503.3 4.4 collective-permute-done.38
  509.2 2.2 collective-permute-start.45
  513.1 3.0 collective-permute-done.44
  516.1 3.2 collective-permute-start.47
  519.3 1.9 collective-permute-start.46
  521.4 3.2 collective-permute-done.46
  525.8 1.5 fusion.41
  528.4 20.9 %reduce-scatter.2.cloned.1.call-done = f32[4,8,8,512]{3,2,1,0:T(8,128)} async-done(((f32[4,8,8,1024]{3,2,1,0:T(8,128)}), f32[4,8,8,512]{3,2,1,0:T(8,128)}) %reduce-scatter.2.cloned.1.call-update) | async-done | bytes 524304 | tf_op jit(solution)/shard_map/reduce_scatter | solution.py:112
  (138 shorter events, 48.2 us)
Async XLA Ops:
  7.2 9.1 %copy-start = (f32[1,4,8,8,1024]{4,3,2,1,0:T(8,128)S(1)}, f32[1,4,8,8,1024]{4,3,2,1,0:T(8,128)}, u32[]{:S(2)}) copy-start(f32[1,4,8,8,1024]{4,3,2,1,0:T(8,128)} %param.11) | copy-start | bytes 3145732
  7.2 18.6 %copy-start.6 = (f32[256,4]{0,1:T(4,128)S(1)}, f32[256,4]{0,1:T(4,128)}, u32[]{:S(2)}) copy-start(f32[256,4]{0,1:T(4,128)} %param.15) | copy-start | bytes 12292
  7.2 19.2 %copy-start.5 = (s32[256,3]{0,1:T(4,128)S(1)}, s32[256,3]{0,1:T(4,128)}, u32[]{:S(2)}) copy-start(s32[256,3]{0,1:T(4,128)} %param.14) | copy-start | bytes 9220
  7.2 19.7 %copy-start.7 = (s32[256,3]{0,1:T(4,128)S(1)}, s32[256,3]{0,1:T(4,128)}, u32[]{:S(2)}) copy-start(s32[256,3]{0,1:T(4,128)} %param.13) | copy-start | bytes 9220
  7.2 542.1 %reduce-scatter.2.cloned.1.call-start = ((), (), s32[]{:S(2)}) async-start(), calls=%async_computation.1 | async-start | bytes 1572864 | tf_op jit(solution)/shard_map/reduce_scatter | solution.py:112
  9.7 335.5 %collective-permute-start.5 = (bf16[4,1,8,1024]{3,2,1,0:T(8,128)(2,1)}, bf16[4,1,8,1024]{3,2,1,0:T(8,128)(2,1)}, u32[]{:S(2)}, u32[]{:S(2)}) collective-permute-start(bf16[4,1,8,1024]{3,2,1,0:T(8,128)(2,1)} %get-tuple-element.83), channel_id=1, source_target_pairs={{8,0},{16,8},{24,16},{32,24},{40,32},{48,40},{56,48},{9,1},{17,9},... | collective-permute-start | bytes 196616 | tf_op jit(solution)/shard_map/ppermute | solution.py:17
  11.0 335.5 %collective-permute-start.4 = (bf16[4,1,8,1024]{3,2,1,0:T(8,128)(2,1)}, bf16[4,1,8,1024]{3,2,1,0:T(8,128)(2,1)}, u32[]{:S(2)}, u32[]{:S(2)}) collective-permute-start(bf16[4,1,8,1024]{3,2,1,0:T(8,128)(2,1)} %get-tuple-element.82), channel_id=1, source_target_pairs={{0,8},{8,16},{16,24},{24,32},{32,40},{40,48},{48,56},{1,9},{9,17},... | collective-permute-start | bytes 196616 | tf_op jit(solution)/shard_map/ppermute | solution.py:16
  17.0 357.2 %collective-permute-start.1 = (f32[4,1,8,1024]{3,2,1,0:T(8,128)}, f32[4,1,8,1024]{3,2,1,0:T(8,128)S(1)}, u32[]{:S(2)}, u32[]{:S(2)}) collective-permute-start(f32[4,1,8,1024]{3,2,1,0:T(8,128)} %get-tuple-element.66), channel_id=1, source_target_pairs={{0,8},{8,16},{16,24},{24,32},{32,40},{40,48},{48,56},{1,9},{9,17},... | collective-permute-start | bytes 393224 | tf_op jit(solution)/shard_map/ppermute | solution.py:16
  20.6 356.7 %collective-permute-start = (f32[4,1,8,1024]{3,2,1,0:T(8,128)}, f32[4,1,8,1024]{3,2,1,0:T(8,128)}, u32[]{:S(2)}, u32[]{:S(2)}) collective-permute-start(f32[4,1,8,1024]{3,2,1,0:T(8,128)} %get-tuple-element.67), channel_id=1, source_target_pairs={{8,0},{16,8},{24,16},{32,24},{40,32},{48,40},{56,48},{9,1},{17,9},... | collective-permute-start | bytes 393224 | tf_op jit(solution)/shard_map/ppermute | solution.py:17
  22.6 326.4 %collective-permute-start.17 = (bf16[4,1,8,1024]{3,2,1,0:T(8,128)(2,1)}, bf16[4,1,8,1024]{3,2,1,0:T(8,128)(2,1)}, u32[]{:S(2)}, u32[]{:S(2)}) collective-permute-start(bf16[4,1,8,1024]{3,2,1,0:T(8,128)(2,1)} %get-tuple-element.81), channel_id=1, source_target_pairs={{8,0},{16,8},{24,16},{32,24},{40,32},{48,40},{56,48},{9,1},{17,9},... | collective-permute-start | bytes 196616 | tf_op jit(solution)/shard_map/ppermute | solution.py:17
  345.2 7.8 %collective-permute-start.16 = (bf16[4,1,8,1024]{3,2,1,0:T(8,128)(2,1)}, bf16[4,1,8,1024]{3,2,1,0:T(8,128)(2,1)S(1)}, u32[]{:S(2)}, u32[]{:S(2)}) collective-permute-start(bf16[4,1,8,1024]{3,2,1,0:T(8,128)(2,1)} %get-tuple-element.80), channel_id=1, source_target_pairs={{0,8},{8,16},{16,24},{24,32},{32,40},{40,48},{48,56},{1,9},{9,17},... | collective-permute-start | bytes 196616 | tf_op jit(solution)/shard_map/ppermute | solution.py:16
  346.5 8.9 %collective-permute-start.29 = (bf16[4,1,8,1024]{3,2,1,0:T(8,128)(2,1)}, bf16[4,1,8,1024]{3,2,1,0:T(8,128)(2,1)S(1)}, u32[]{:S(2)}, u32[]{:S(2)}) collective-permute-start(bf16[4,1,8,1024]{3,2,1,0:T(8,128)(2,1)} %get-tuple-element.79), channel_id=1, source_target_pairs={{8,0},{16,8},{24,16},{32,24},{40,32},{48,40},{56,48},{9,1},{17,9},... | collective-permute-start | bytes 196616 | tf_op jit(solution)/shard_map/ppermute | solution.py:17
  349.0 10.5 %collective-permute-start.28 = (bf16[4,1,8,1024]{3,2,1,0:T(8,128)(2,1)}, bf16[4,1,8,1024]{3,2,1,0:T(8,128)(2,1)S(1)}, u32[]{:S(2)}, u32[]{:S(2)}) collective-permute-start(bf16[4,1,8,1024]{3,2,1,0:T(8,128)(2,1)} %get-tuple-element.78), channel_id=1, source_target_pairs={{0,8},{8,16},{16,24},{24,32},{32,40},{40,48},{48,56},{1,9},{9,17},... | collective-permute-start | bytes 196616 | tf_op jit(solution)/shard_map/ppermute | solution.py:16
  353.0 16.6 %collective-permute-start.41 = (bf16[4,1,8,1024]{3,2,1,0:T(8,128)(2,1)}, bf16[4,1,8,1024]{3,2,1,0:T(8,128)(2,1)S(1)}, u32[]{:S(2)}, u32[]{:S(2)}) collective-permute-start(bf16[4,1,8,1024]{3,2,1,0:T(8,128)(2,1)} %get-tuple-element.77), channel_id=1, source_target_pairs={{8,0},{16,8},{24,16},{32,24},{40,32},{48,40},{56,48},{9,1},{17,9},... | collective-permute-start | bytes 196616 | tf_op jit(solution)/shard_map/ppermute | solution.py:17
  355.5 16.0 %collective-permute-start.40 = (bf16[4,1,8,1024]{3,2,1,0:T(8,128)(2,1)}, bf16[4,1,8,1024]{3,2,1,0:T(8,128)(2,1)S(1)}, u32[]{:S(2)}, u32[]{:S(2)}) collective-permute-start(bf16[4,1,8,1024]{3,2,1,0:T(8,128)(2,1)} %get-tuple-element.76), channel_id=1, source_target_pairs={{0,8},{8,16},{16,24},{24,32},{32,40},{40,48},{48,56},{1,9},{9,17},... | collective-permute-start | bytes 196616 | tf_op jit(solution)/shard_map/ppermute | solution.py:16
  359.5 21.0 %collective-permute-start.7 = (bf16[4,10,1,1024]{3,2,1,0:T(2,128)(2,1)S(1)}, bf16[4,10,1,1024]{3,2,1,0:T(2,128)(2,1)S(1)}, u32[]{:S(2)}, u32[]{:S(2)}) collective-permute-start(bf16[4,10,1,1024]{3,2,1,0:T(2,128)(2,1)S(1)} %get-tuple-element.75), channel_id=1, source_target_pairs={{1,0},{2,1},{3,2},{4,3},{5,4},{6,5},{7,6},{9,8},{10,9},{11,10},{12... | collective-permute-start | bytes 245768 | tf_op jit(solution)/shard_map/ppermute | solution.py:17
  369.6 14.5 %collective-permute-start.6 = (bf16[4,10,1,1024]{3,2,1,0:T(2,128)(2,1)S(1)}, bf16[4,10,1,1024]{3,2,1,0:T(2,128)(2,1)S(1)}, u32[]{:S(2)}, u32[]{:S(2)}) collective-permute-start(bf16[4,10,1,1024]{3,2,1,0:T(2,128)(2,1)S(1)} %get-tuple-element.74), channel_id=1, source_target_pairs={{0,1},{1,2},{2,3},{3,4},{4,5},{5,6},{6,7},{8,9},{9,10},{10,11},{11... | collective-permute-start | bytes 245768 | tf_op jit(solution)/shard_map/ppermute | solution.py:16
  371.5 25.6 %collective-permute-start.19 = (bf16[4,10,1,1024]{3,2,1,0:T(2,128)(2,1)S(1)}, bf16[4,10,1,1024]{3,2,1,0:T(2,128)(2,1)S(1)}, u32[]{:S(2)}, u32[]{:S(2)}) collective-permute-start(bf16[4,10,1,1024]{3,2,1,0:T(2,128)(2,1)S(1)} %get-tuple-element.73), channel_id=1, source_target_pairs={{1,0},{2,1},{3,2},{4,3},{5,4},{6,5},{7,6},{9,8},{10,9},{11,10},{12... | collective-permute-start | bytes 245768 | tf_op jit(solution)/shard_map/ppermute | solution.py:17
  374.2 25.5 %collective-permute-start.18 = (bf16[4,10,1,1024]{3,2,1,0:T(2,128)(2,1)S(1)}, bf16[4,10,1,1024]{3,2,1,0:T(2,128)(2,1)S(1)}, u32[]{:S(2)}, u32[]{:S(2)}) collective-permute-start(bf16[4,10,1,1024]{3,2,1,0:T(2,128)(2,1)S(1)} %get-tuple-element.72), channel_id=1, source_target_pairs={{0,1},{1,2},{2,3},{3,4},{4,5},{5,6},{6,7},{8,9},{9,10},{10,11},{11... | collective-permute-start | bytes 245768 | tf_op jit(solution)/shard_map/ppermute | solution.py:16
  377.3 50.0 %collective-permute-start.31 = (bf16[4,10,1,1024]{3,2,1,0:T(2,128)(2,1)S(1)}, bf16[4,10,1,1024]{3,2,1,0:T(2,128)(2,1)S(1)}, u32[]{:S(2)}, u32[]{:S(2)}) collective-permute-start(bf16[4,10,1,1024]{3,2,1,0:T(2,128)(2,1)S(1)} %get-tuple-element.71), channel_id=1, source_target_pairs={{1,0},{2,1},{3,2},{4,3},{5,4},{6,5},{7,6},{9,8},{10,9},{11,10},{12... | collective-permute-start | bytes 245768 | tf_op jit(solution)/shard_map/ppermute | solution.py:17
  380.5 8.6 %collective-permute-start.3 = (f32[4,10,1,1024]{3,2,1,0:T(1,128)S(1)}, f32[4,10,1,1024]{3,2,1,0:T(1,128)S(1)}, u32[]{:S(2)}, u32[]{:S(2)}) collective-permute-start(f32[4,10,1,1024]{3,2,1,0:T(1,128)S(1)} %get-tuple-element.47), channel_id=1, source_target_pairs={{0,1},{1,2},{2,3},{3,4},{4,5},{5,6},{6,7},{8,9},{9,10},{10,11},{11... | collective-permute-start | bytes 491528 | tf_op jit(solution)/shard_map/ppermute | solution.py:16
  384.1 8.7 %collective-permute-start.2 = (f32[4,10,1,1024]{3,2,1,0:T(1,128)S(1)}, f32[4,10,1,1024]{3,2,1,0:T(1,128)S(1)}, u32[]{:S(2)}, u32[]{:S(2)}) collective-permute-start(f32[4,10,1,1024]{3,2,1,0:T(1,128)S(1)} %get-tuple-element.46), channel_id=1, source_target_pairs={{1,0},{2,1},{3,2},{4,3},{5,4},{6,5},{7,6},{9,8},{10,9},{11,10},{12... | collective-permute-start | bytes 491528 | tf_op jit(solution)/shard_map/ppermute | solution.py:17
  389.0 7.7 %copy-start.1 = (f32[8,8,1024]{2,1,0:T(8,128)S(1)}, f32[8,8,1024]{2,1,0:T(8,128)}, u32[]{:S(2)}) copy-start(f32[8,8,1024]{2,1,0:T(8,128)} %param.8) | copy-start | bytes 786436
  389.0 7.7 %copy-start.4 = (f32[8,8,1024]{2,1,0:T(8,128)S(1)}, f32[8,8,1024]{2,1,0:T(8,128)}, u32[]{:S(2)}) copy-start(f32[8,8,1024]{2,1,0:T(8,128)} %reshape.127) | copy-start | bytes 786436
  389.1 40.2 %collective-permute-start.30 = (bf16[4,10,1,1024]{3,2,1,0:T(2,128)(2,1)S(1)}, bf16[4,10,1,1024]{3,2,1,0:T(2,128)(2,1)S(1)}, u32[]{:S(2)}, u32[]{:S(2)}) collective-permute-start(bf16[4,10,1,1024]{3,2,1,0:T(2,128)(2,1)S(1)} %get-tuple-element.70), channel_id=1, source_target_pairs={{0,1},{1,2},{2,3},{3,4},{4,5},{5,6},{6,7},{8,9},{9,10},{10,11},{11... | collective-permute-start | bytes 245768 | tf_op jit(solution)/shard_map/ppermute | solution.py:16
  392.9 54.9 %collective-permute-start.43 = (bf16[4,10,1,1024]{3,2,1,0:T(2,128)(2,1)S(1)}, bf16[4,10,1,1024]{3,2,1,0:T(2,128)(2,1)S(1)}, u32[]{:S(2)}, u32[]{:S(2)}) collective-permute-start(bf16[4,10,1,1024]{3,2,1,0:T(2,128)(2,1)S(1)} %get-tuple-element.69), channel_id=1, source_target_pairs={{1,0},{2,1},{3,2},{4,3},{5,4},{6,5},{7,6},{9,8},{10,9},{11,10},{12... | collective-permute-start | bytes 245768 | tf_op jit(solution)/shard_map/ppermute | solution.py:17
  397.1 5.4 collective-permute-start.9
  399.6 4.7 collective-permute-start.8
  404.4 7.6 %collective-permute-start.11 = (f32[10,1,1024]{2,1,0:T(1,128)S(1)}, f32[10,1,1024]{2,1,0:T(1,128)S(1)}, u32[]{:S(2)}, u32[]{:S(2)}) collective-permute-start(f32[10,1,1024]{2,1,0:T(1,128)S(1)} %get-tuple-element.99), channel_id=1, source_target_pairs={{0,1},{1,2},{2,3},{3,4},{4,5},{5,6},{6,7},{8,9},{9,10},{10,11},{11... | collective-permute-start | bytes 122888 | tf_op jit(solution)/shard_map/ppermute | solution.py:16
  409.4 5.3 collective-permute-start.10
  415.5 4.5 collective-permute-start.13
  418.0 5.7 %collective-permute-start.12 = (f32[4,1,8,1024]{3,2,1,0:T(8,128)S(1)}, f32[4,1,8,1024]{3,2,1,0:T(8,128)S(1)}, u32[]{:S(2)}, u32[]{:S(2)}) collective-permute-start(f32[4,1,8,1024]{3,2,1,0:T(8,128)S(1)} %get-tuple-element.62), channel_id=1, source_target_pairs={{8,0},{16,8},{24,16},{32,24},{40,32},{48,40},{56,48},{9,1},{17,9},... | collective-permute-start | bytes 393224 | tf_op jit(solution)/shard_map/ppermute | solution.py:17
  420.0 27.8 %collective-permute-start.42 = (bf16[4,10,1,1024]{3,2,1,0:T(2,128)(2,1)S(1)}, bf16[4,10,1,1024]{3,2,1,0:T(2,128)(2,1)S(1)}, u32[]{:S(2)}, u32[]{:S(2)}) collective-permute-start(bf16[4,10,1,1024]{3,2,1,0:T(2,128)(2,1)S(1)} %get-tuple-element.68), channel_id=1, source_target_pairs={{0,1},{1,2},{2,3},{3,4},{4,5},{5,6},{6,7},{8,9},{9,10},{10,11},{11... | collective-permute-start | bytes 245768 | tf_op jit(solution)/shard_map/ppermute | solution.py:16
  423.9 6.0 %collective-permute-start.15 = (f32[4,10,1,1024]{3,2,1,0:T(1,128)S(1)}, f32[4,10,1,1024]{3,2,1,0:T(1,128)S(1)}, u32[]{:S(2)}, u32[]{:S(2)}) collective-permute-start(f32[4,10,1,1024]{3,2,1,0:T(1,128)S(1)} %get-tuple-element.43), channel_id=1, source_target_pairs={{0,1},{1,2},{2,3},{3,4},{4,5},{5,6},{6,7},{8,9},{9,10},{10,11},{11... | collective-permute-start | bytes 491528 | tf_op jit(solution)/shard_map/ppermute | solution.py:16
  427.3 6.6 %collective-permute-start.14 = (f32[4,10,1,1024]{3,2,1,0:T(1,128)S(1)}, f32[4,10,1,1024]{3,2,1,0:T(1,128)S(1)}, u32[]{:S(2)}, u32[]{:S(2)}) collective-permute-start(f32[4,10,1,1024]{3,2,1,0:T(1,128)S(1)} %get-tuple-element.42), channel_id=1, source_target_pairs={{1,0},{2,1},{3,2},{4,3},{5,4},{6,5},{7,6},{9,8},{10,9},{11,10},{12... | collective-permute-start | bytes 491528 | tf_op jit(solution)/shard_map/ppermute | solution.py:17
  429.9 5.1 copy-start.3
  435.4 4.5 collective-permute-start.21
  437.9 4.7 collective-permute-start.20
  442.6 5.8 %collective-permute-start.23 = (f32[10,1,1024]{2,1,0:T(1,128)S(1)}, f32[10,1,1024]{2,1,0:T(1,128)S(1)}, u32[]{:S(2)}, u32[]{:S(2)}) collective-permute-start(f32[10,1,1024]{2,1,0:T(1,128)S(1)} %get-tuple-element.95), channel_id=1, source_target_pairs={{0,1},{1,2},{2,3},{3,4},{4,5},{5,6},{6,7},{8,9},{9,10},{10,11},{11... | collective-permute-start | bytes 122888 | tf_op jit(solution)/shard_map/ppermute | solution.py:16
  445.8 5.3 collective-permute-start.22
  451.9 4.5 collective-permute-start.25
  454.4 5.7 %collective-permute-start.24 = (f32[4,1,8,1024]{3,2,1,0:T(8,128)S(1)}, f32[4,1,8,1024]{3,2,1,0:T(8,128)S(1)}, u32[]{:S(2)}, u32[]{:S(2)}) collective-permute-start(f32[4,1,8,1024]{3,2,1,0:T(8,128)S(1)} %get-tuple-element.57), channel_id=1, source_target_pairs={{8,0},{16,8},{24,16},{32,24},{40,32},{48,40},{56,48},{9,1},{17,9},... | collective-permute-start | bytes 393224 | tf_op jit(solution)/shard_map/ppermute | solution.py:17
  460.3 6.7 %collective-permute-start.27 = (f32[4,10,1,1024]{3,2,1,0:T(1,128)S(1)}, f32[4,10,1,1024]{3,2,1,0:T(1,128)S(1)}, u32[]{:S(2)}, u32[]{:S(2)}) collective-permute-start(f32[4,10,1,1024]{3,2,1,0:T(1,128)S(1)} %get-tuple-element.39), channel_id=1, source_target_pairs={{0,1},{1,2},{2,3},{3,4},{4,5},{5,6},{6,7},{8,9},{9,10},{10,11},{11... | collective-permute-start | bytes 491528 | tf_op jit(solution)/shard_map/ppermute | solution.py:16
  463.7 6.6 %collective-permute-start.26 = (f32[4,10,1,1024]{3,2,1,0:T(1,128)S(1)}, f32[4,10,1,1024]{3,2,1,0:T(1,128)S(1)}, u32[]{:S(2)}, u32[]{:S(2)}) collective-permute-start(f32[4,10,1,1024]{3,2,1,0:T(1,128)S(1)} %get-tuple-element.38), channel_id=1, source_target_pairs={{1,0},{2,1},{3,2},{4,3},{5,4},{6,5},{7,6},{9,8},{10,9},{11,10},{12... | collective-permute-start | bytes 491528 | tf_op jit(solution)/shard_map/ppermute | solution.py:17
  467.0 4.4 copy-start.2
  471.8 4.2 collective-permute-start.33
  474.4 4.7 collective-permute-start.32
  479.1 5.3 collective-permute-start.35
  482.3 5.3 collective-permute-start.34
  488.3 4.5 collective-permute-start.37
  490.9 5.7 %collective-permute-start.36 = (f32[4,1,8,1024]{3,2,1,0:T(8,128)S(1)}, f32[4,1,8,1024]{3,2,1,0:T(8,128)S(1)}, u32[]{:S(2)}, u32[]{:S(2)}) collective-permute-start(f32[4,1,8,1024]{3,2,1,0:T(8,128)S(1)} %get-tuple-element.52), channel_id=1, source_target_pairs={{8,0},{16,8},{24,16},{32,24},{40,32},{48,40},{56,48},{9,1},{17,9},... | collective-permute-start | bytes 393224 | tf_op jit(solution)/shard_map/ppermute | solution.py:17
  496.8 6.6 %collective-permute-start.39 = (f32[4,10,1,1024]{3,2,1,0:T(1,128)S(1)}, f32[4,10,1,1024]{3,2,1,0:T(1,128)S(1)}, u32[]{:S(2)}, u32[]{:S(2)}) collective-permute-start(f32[4,10,1,1024]{3,2,1,0:T(1,128)S(1)} %get-tuple-element.35), channel_id=1, source_target_pairs={{0,1},{1,2},{2,3},{3,4},{4,5},{5,6},{6,7},{8,9},{9,10},{10,11},{11... | collective-permute-start | bytes 491528 | tf_op jit(solution)/shard_map/ppermute | solution.py:16
  501.1 6.6 %collective-permute-start.38 = (f32[4,10,1,1024]{3,2,1,0:T(1,128)S(1)}, f32[4,10,1,1024]{3,2,1,0:T(1,128)S(1)}, u32[]{:S(2)}, u32[]{:S(2)}) collective-permute-start(f32[4,10,1,1024]{3,2,1,0:T(1,128)S(1)} %get-tuple-element.34), channel_id=1, source_target_pairs={{1,0},{2,1},{3,2},{4,3},{5,4},{6,5},{7,6},{9,8},{10,9},{11,10},{12... | collective-permute-start | bytes 491528 | tf_op jit(solution)/shard_map/ppermute | solution.py:17
  509.2 3.9 collective-permute-start.45
  511.4 4.7 collective-permute-start.44
  516.1 5.3 collective-permute-start.47
  519.3 5.3 collective-permute-start.46
Sparse Core Ops, SparseCore 0:
  527.4 21.7 reduce-scatter.1
where the time goes:
time: 559 us; the launch traced here: 556 us
  blocking collectives  279 us (50%)
  starting transfers between devices  124 us (22%)
  waiting for transfers between devices  64.3 us (12%)
  other arithmetic  39.6 us (7%)
  local copies, waits for them, and re-layouts  33.9 us (6%)
  between operations  15.8 us (3%)
    psum x1, blocking collectives, shards(): samples = lax.psum(local_samples, ('gx', 'gy'))  279 us
    ppermute x24, starting transfers between devices, extended(): before = lax.ppermute(last, axis, up)  76.4 us
    ppermute x24, starting transfers between devices, extended(): after = lax.ppermute(initial, axis, down)  47.4 us
    ppermute x24, waiting for transfers between devices, extended(): after = lax.ppermute(initial, axis, down)  42.7 us
    reduce_scatter x1, waiting for transfers between devices, shards(): lax.psum_scatter(kernel_local, 'pair', scatter_dimension=3, tiled=True)  20.9 us
    slice x2, local copies, waits for them, and re-layouts, shards(): pressure_snaps = forward_field[:, 0].reshape(steps_total, -1)  14.9 us
  transfers between devices with their start and end apart: 49, of which 18 were waited for; matrix products, arithmetic and copies ran while one was open for 11% of the time, Pallas kernels for 0%

commit v1 on v0

--- a/solution.py
+++ b/solution.py
@@ -62,7 +62,13 @@
     local_samples = (
         jnp.take(pressure_snaps, src_flat, axis=1).astype(jnp.float32) * src_inside[None, :]
     )
-    samples = lax.psum(local_samples, ("gx", "gy"))
+
+    def _play_cells(x_part, which_axis, shard_axis):
+        for pp in (which_axis, shard_axis):
+            x_part = jax.lax.psum(x_part, pp)
+        return x_part
+
+    samples = _play_cells(local_samples, "gy", "gx")
     state = adjoint_state[0]
     kernel_local = jnp.zeros((4, width_x, width_y, depth), jnp.float32)
     for step in range(steps_total):

time: 559 us -> 348 us (0.62)
  blocking collectives: 279 us -> 57.5 us
  starting transfers between devices: 124 us -> 134 us
    psum x1 -> x2, blocking collectives: 279 us -> 57.5 us  [_play_cells(): x_part = jax.lax.psum(x_part, pp)]
    ppermute x24, starting transfers between devices: 76.4 us -> 83.2 us  [extended(): before = lax.ppermute(last, axis, up)]
  transfers between devices with their start and end apart: 49 -> 49, of which waited for: 18 -> 18; matrix products, arithmetic and copies ran while one was open for 11% -> 18% of each run, Pallas kernels for 0% -> 0%
where the time goes in v1:
time: 348 us; the launch traced here: 344 us
  starting transfers between devices  134 us (39%)
  waiting for transfers between devices  63.1 us (18%)
  blocking collectives  57.5 us (17%)
  other arithmetic  39.7 us (11%)
  local copies, waits for them, and re-layouts  34 us (10%)
  between operations  15.8 us (5%)
    ppermute x24, starting transfers between devices, extended(): before = lax.ppermute(last, axis, up)  83.2 us
    psum x2, blocking collectives, _play_cells(): x_part = jax.lax.psum(x_part, pp)  57.5 us
    ppermute x24, starting transfers between devices, extended(): after = lax.ppermute(initial, axis, down)  51.2 us
    ppermute x24, waiting for transfers between devices, extended(): after = lax.ppermute(initial, axis, down)  43.3 us
    reduce_scatter x1, waiting for transfers between devices, shards(): lax.psum_scatter(kernel_local, 'pair', scatter_dimension=3, tiled=True)  19.1 us
    slice x2, local copies, waits for them, and re-layouts, shards(): pressure_snaps = forward_field[:, 0].reshape(steps_total, -1)  15 us
    scatter-add x4, other arithmetic, shards(): injected = jnp.zeros((width_x * width_y * depth,), jnp.float32).at[rcv_fl...  9.35 us
    gather x1, local copies, waits for them, and re-layouts, shards(): jnp.take(pressure_snaps, src_flat, axis=1).astype(jnp.float32)  8.65 us
  transfers between devices with their start and end apart: 49, of which 18 were waited for; matrix products, arithmetic and copies ran while one was open for 18% of the time, Pallas kernels for 0%

profile of v1, /device:TPU:1, one launch (start us, length us, event | category | flops | bytes accessed | tf_op | source)
XLA Modules:
  0.0 344.5 jit_solution(7690591108701648118)
XLA Ops:
  7.2 1.8 slice_bitcast_fusion
  11.0 5.2 %collective-permute-start.4 = (bf16[4,1,8,1024]{3,2,1,0:T(8,128)(2,1)}, bf16[4,1,8,1024]{3,2,1,0:T(8,128)(2,1)}, u32[]{:S(2)}, u32[]{:S(2)}) collective-permute-start(bf16[4,1,8,1024]{3,2,1,0:T(8,128)(2,1)} %get-tuple-element.82), channel_id=1, source_target_pairs={{0,8},{8,16},{16,24},{24,32},{32,40},{40,48},{48,56},{1,9},{9,17},... | collective-permute-start | bytes 196616 | tf_op jit(solution)/shard_map/ppermute | solution.py:16
  17.0 3.6 %collective-permute-start.1 = (f32[4,1,8,1024]{3,2,1,0:T(8,128)}, f32[4,1,8,1024]{3,2,1,0:T(8,128)S(1)}, u32[]{:S(2)}, u32[]{:S(2)}) collective-permute-start(f32[4,1,8,1024]{3,2,1,0:T(8,128)} %get-tuple-element.66), channel_id=1, source_target_pairs={{0,8},{8,16},{16,24},{24,32},{32,40},{40,48},{48,56},{1,9},{9,17},... | collective-permute-start | bytes 393224 | tf_op jit(solution)/shard_map/ppermute | solution.py:16
  23.9 1.9 slice.831
  26.9 13.2 %copy.11 = bf16[4,1,8,8,1024]{0,4,3,2,1:T(8,128)(2,1)} copy(bf16[4,1,8,8,1024]{4,3,2,1,0:T(8,128)(2,1)} %slice.831) | data formatting | bytes 1048576 | tf_op jit(solution)/shard_map/slice | solution.py:61
  40.1 8.7 %gather_fusion = bf16[256,4]{1,0:T(8,128)(2,1)S(1)} fusion(bf16[4,65536]{0,1:T(8,128)(2,1)} %bitcast.532, s32[1024]{0:T(1024)S(1)} %pad_clamp_fusion), kind=kCustom, calls=%fused_computation | custom fusion | bytes 5120 | tf_op jit(solution)/shard_map/jit(_take)/gather | solution.py:63
  48.9 25.2 %psum.14 = f32[4,256]{0,1:T(8,128)S(1)} all-reduce(f32[4,256]{0,1:T(8,128)S(1)} %multiply_bitcast_fusion), channel_id=1, replica_groups=mesh['pair'=2,'gx'=8,'gy'=8] {'gy'}, use_global_device_ids=true, to_apply=%region_0.1 | all-reduce | flops 1024 | bytes 8192 | tf_op jit(solution)/shard_map/psum | solution.py:68
  74.2 32.2 %psum.15 = f32[4,256]{0,1:T(8,128)S(1)} all-reduce(f32[4,256]{0,1:T(8,128)S(1)} %psum.14), channel_id=1, replica_groups=mesh['pair'=2,'gx'=8,'gy'=8] {'gx'}, use_global_device_ids=true, to_apply=%region_1.2 | all-reduce | flops 1024 | bytes 8192 | tf_op jit(solution)/shard_map/psum | solution.py:68
  109.6 1.3 select_select_fusion
  111.5 2.2 scatter_custom_fusion
  114.4 2.2 scatter_custom_fusion.1
  117.3 2.2 scatter_custom_fusion.2
  120.3 2.8 scatter_custom_fusion.3
  127.9 4.0 %collective-permute-start.28 = (bf16[4,1,8,1024]{3,2,1,0:T(8,128)(2,1)}, bf16[4,1,8,1024]{3,2,1,0:T(8,128)(2,1)S(1)}, u32[]{:S(2)}, u32[]{:S(2)}) collective-permute-start(bf16[4,1,8,1024]{3,2,1,0:T(8,128)(2,1)} %get-tuple-element.78), channel_id=1, source_target_pairs={{0,8},{8,16},{16,24},{24,32},{32,40},{40,48},{48,56},{1,9},{9,17},... | collective-permute-start | bytes 196616 | tf_op jit(solution)/shard_map/ppermute | solution.py:16
  134.3 4.3 %collective-permute-start.40 = (bf16[4,1,8,1024]{3,2,1,0:T(8,128)(2,1)}, bf16[4,1,8,1024]{3,2,1,0:T(8,128)(2,1)S(1)}, u32[]{:S(2)}, u32[]{:S(2)}) collective-permute-start(bf16[4,1,8,1024]{3,2,1,0:T(8,128)(2,1)} %get-tuple-element.76), channel_id=1, source_target_pairs={{0,8},{8,16},{16,24},{24,32},{32,40},{40,48},{48,56},{1,9},{9,17},... | collective-permute-start | bytes 196616 | tf_op jit(solution)/shard_map/ppermute | solution.py:16
  138.7 13.7 %collective-permute-start.7 = (bf16[4,10,1,1024]{3,2,1,0:T(2,128)(2,1)S(1)}, bf16[4,10,1,1024]{3,2,1,0:T(2,128)(2,1)S(1)}, u32[]{:S(2)}, u32[]{:S(2)}) collective-permute-start(bf16[4,10,1,1024]{3,2,1,0:T(2,128)(2,1)S(1)} %get-tuple-element.75), channel_id=1, source_target_pairs={{1,0},{2,1},{3,2},{4,3},{5,4},{6,5},{7,6},{9,8},{10,9},{11,10},{12... | collective-permute-start | bytes 245768 | tf_op jit(solution)/shard_map/ppermute | solution.py:17
  152.6 1.9 collective-permute-start.6
  154.6 2.4 collective-permute-start.19
  157.2 3.2 collective-permute-start.18
  160.4 1.9 collective-permute-start.31
  163.5 3.6 %collective-permute-start.3 = (f32[4,10,1,1024]{3,2,1,0:T(1,128)S(1)}, f32[4,10,1,1024]{3,2,1,0:T(1,128)S(1)}, u32[]{:S(2)}, u32[]{:S(2)}) collective-permute-start(f32[4,10,1,1024]{3,2,1,0:T(1,128)S(1)} %get-tuple-element.47), channel_id=1, source_target_pairs={{0,1},{1,2},{2,3},{3,4},{4,5},{5,6},{6,7},{8,9},{9,10},{10,11},{11... | collective-permute-start | bytes 491528 | tf_op jit(solution)/shard_map/ppermute | solution.py:16
  167.2 2.1 collective-permute-start.2
  169.3 1.6 maximum_convert_fusion
  172.1 3.8 %collective-permute-start.30 = (bf16[4,10,1,1024]{3,2,1,0:T(2,128)(2,1)S(1)}, bf16[4,10,1,1024]{3,2,1,0:T(2,128)(2,1)S(1)}, u32[]{:S(2)}, u32[]{:S(2)}) collective-permute-start(bf16[4,10,1,1024]{3,2,1,0:T(2,128)(2,1)S(1)} %get-tuple-element.70), channel_id=1, source_target_pairs={{0,1},{1,2},{2,3},{3,4},{4,5},{5,6},{6,7},{8,9},{9,10},{10,11},{11... | collective-permute-start | bytes 245768 | tf_op jit(solution)/shard_map/ppermute | solution.py:16
  175.9 1.9 collective-permute-start.43
  177.8 1.9 fusion.39
  180.1 4.3 %collective-permute-start.9 = (f32[1,8,1024]{2,1,0:T(8,128)S(1)}, f32[1,8,1024]{2,1,0:T(8,128)S(1)}, u32[]{:S(2)}, u32[]{:S(2)}) collective-permute-start(f32[1,8,1024]{2,1,0:T(8,128)S(1)} %get-tuple-element.110), channel_id=1, source_target_pairs={{0,8},{8,16},{16,24},{24,32},{32,40},{40,48},{48,56},{1,9},{9,17},... | collective-permute-start | bytes 98312 | tf_op jit(solution)/shard_map/ppermute | solution.py:16
  185.8 1.5 maximum_convert_fusion.1
  187.3 1.8 collective-permute-done.8
  189.2 5.1 %collective-permute-start.11 = (f32[10,1,1024]{2,1,0:T(1,128)S(1)}, f32[10,1,1024]{2,1,0:T(1,128)S(1)}, u32[]{:S(2)}, u32[]{:S(2)}) collective-permute-start(f32[10,1,1024]{2,1,0:T(1,128)S(1)} %get-tuple-element.99), channel_id=1, source_target_pairs={{0,1},{1,2},{2,3},{3,4},{4,5},{5,6},{6,7},{8,9},{9,10},{10,11},{11... | collective-permute-start | bytes 122888 | tf_op jit(solution)/shard_map/ppermute | solution.py:16
  194.3 1.9 collective-permute-start.10
  196.8 2.8 collective-permute-done.10
  200.3 2.5 collective-permute-start.13
  204.8 2.7 collective-permute-start.42
  208.8 3.3 collective-permute-start.15
  212.1 1.9 collective-permute-start.14
  214.8 4.0 %collective-permute-done.14 = f32[4,10,1,1024]{3,2,1,0:T(1,128)S(1)} collective-permute-done((f32[4,10,1,1024]{3,2,1,0:T(1,128)S(1)}, f32[4,10,1,1024]{3,2,1,0:T(1,128)S(1)}, u32[]{:S(2)}, u32[]{:S(2)}) %collective-permute-start.14) | collective-permute-done | bytes 163872 | tf_op jit(solution)/shard_map/ppermute | solution.py:17
  220.2 3.6 %collective-permute-start.21 = (f32[1,8,1024]{2,1,0:T(8,128)S(1)}, f32[1,8,1024]{2,1,0:T(8,128)S(1)}, u32[]{:S(2)}, u32[]{:S(2)}) collective-permute-start(f32[1,8,1024]{2,1,0:T(8,128)S(1)} %get-tuple-element.107), channel_id=1, source_target_pairs={{0,8},{8,16},{16,24},{24,32},{32,40},{40,48},{48,56},{1,9},{9,17},... | collective-permute-start | bytes 98312 | tf_op jit(solution)/shard_map/ppermute | solution.py:16
  225.7 2.8 collective-permute-done.20
  228.5 3.1 collective-permute-start.23
  231.7 1.9 collective-permute-start.22
  234.3 2.7 collective-permute-done.22
  237.7 4.3 %collective-permute-start.25 = (f32[4,1,8,1024]{3,2,1,0:T(8,128)S(1)}, f32[4,1,8,1024]{3,2,1,0:T(8,128)S(1)}, u32[]{:S(2)}, u32[]{:S(2)}) collective-permute-start(f32[4,1,8,1024]{3,2,1,0:T(8,128)S(1)} %get-tuple-element.56), channel_id=1, source_target_pairs={{0,8},{8,16},{16,24},{24,32},{32,40},{40,48},{48,56},{1,9},{9,17},... | collective-permute-start | bytes 393224 | tf_op jit(solution)/shard_map/ppermute | solution.py:16
  243.9 4.3 %collective-permute-done.24 = f32[4,1,8,1024]{3,2,1,0:T(8,128)S(1)} collective-permute-done((f32[4,1,8,1024]{3,2,1,0:T(8,128)S(1)}, f32[4,1,8,1024]{3,2,1,0:T(8,128)S(1)}, u32[]{:S(2)}, u32[]{:S(2)}) %collective-permute-start.24) | collective-permute-done | bytes 131104 | tf_op jit(solution)/shard_map/ppermute | solution.py:17
  248.5 3.1 collective-permute-start.27
  251.5 2.1 collective-permute-start.26
  254.9 3.2 collective-permute-done.26
  259.6 3.9 %collective-permute-start.33 = (f32[1,8,1024]{2,1,0:T(8,128)S(1)}, f32[1,8,1024]{2,1,0:T(8,128)S(1)}, u32[]{:S(2)}, u32[]{:S(2)}) collective-permute-start(f32[1,8,1024]{2,1,0:T(8,128)S(1)} %get-tuple-element.104), channel_id=1, source_target_pairs={{0,8},{8,16},{16,24},{24,32},{32,40},{40,48},{48,56},{1,9},{9,17},... | collective-permute-start | bytes 98312 | tf_op jit(solution)/shard_map/ppermute | solution.py:16
  265.2 3.0 collective-permute-done.32
  268.3 3.2 collective-permute-start.35
  271.5 1.9 collective-permute-start.34
  273.6 3.2 collective-permute-done.34
  277.5 3.5 %collective-permute-start.37 = (f32[4,1,8,1024]{3,2,1,0:T(8,128)S(1)}, f32[4,1,8,1024]{3,2,1,0:T(8,128)S(1)}, u32[]{:S(2)}, u32[]{:S(2)}) collective-permute-start(f32[4,1,8,1024]{3,2,1,0:T(8,128)S(1)} %get-tuple-element.51), channel_id=1, source_target_pairs={{0,8},{8,16},{16,24},{24,32},{32,40},{40,48},{48,56},{1,9},{9,17},... | collective-permute-start | bytes 393224 | tf_op jit(solution)/shard_map/ppermute | solution.py:16
  282.9 3.8 %collective-permute-done.36 = f32[4,1,8,1024]{3,2,1,0:T(8,128)S(1)} collective-permute-done((f32[4,1,8,1024]{3,2,1,0:T(8,128)S(1)}, f32[4,1,8,1024]{3,2,1,0:T(8,128)S(1)}, u32[]{:S(2)}, u32[]{:S(2)}) %collective-permute-start.36) | collective-permute-done | bytes 131104 | tf_op jit(solution)/shard_map/ppermute | solution.py:17
  286.9 3.8 %collective-permute-start.39 = (f32[4,10,1,1024]{3,2,1,0:T(1,128)S(1)}, f32[4,10,1,1024]{3,2,1,0:T(1,128)S(1)}, u32[]{:S(2)}, u32[]{:S(2)}) collective-permute-start(f32[4,10,1,1024]{3,2,1,0:T(1,128)S(1)} %get-tuple-element.35), channel_id=1, source_target_pairs={{0,1},{1,2},{2,3},{3,4},{4,5},{5,6},{6,7},{8,9},{9,10},{10,11},{11... | collective-permute-start | bytes 491528 | tf_op jit(solution)/shard_map/ppermute | solution.py:16
  290.7 1.9 collective-permute-start.38
  292.9 4.4 %collective-permute-done.38 = f32[4,10,1,1024]{3,2,1,0:T(1,128)S(1)} collective-permute-done((f32[4,10,1,1024]{3,2,1,0:T(1,128)S(1)}, f32[4,10,1,1024]{3,2,1,0:T(1,128)S(1)}, u32[]{:S(2)}, u32[]{:S(2)}) %collective-permute-start.38) | collective-permute-done | bytes 163872 | tf_op jit(solution)/shard_map/ppermute | solution.py:17
  298.8 2.8 collective-permute-start.45
  303.3 3.0 collective-permute-done.44
  306.3 3.2 collective-permute-start.47
  309.5 1.9 collective-permute-start.46
  311.6 3.2 collective-permute-done.46
  316.0 1.5 fusion.41
  318.6 19.1 %reduce-scatter.2.cloned.1.call-done = f32[4,8,8,512]{3,2,1,0:T(8,128)} async-done(((f32[4,8,8,1024]{3,2,1,0:T(8,128)}), f32[4,8,8,512]{3,2,1,0:T(8,128)}) %reduce-scatter.2.cloned.1.call-update) | async-done | bytes 524304 | tf_op jit(solution)/shard_map/reduce_scatter | solution.py:118
  (139 shorter events, 49.6 us)
Async XLA Ops:
  7.2 9.1 %copy-start = (f32[1,4,8,8,1024]{4,3,2,1,0:T(8,128)S(1)}, f32[1,4,8,8,1024]{4,3,2,1,0:T(8,128)}, u32[]{:S(2)}) copy-start(f32[1,4,8,8,1024]{4,3,2,1,0:T(8,128)} %param.11) | copy-start | bytes 3145732
  7.2 18.6 %copy-start.6 = (f32[256,4]{0,1:T(4,128)S(1)}, f32[256,4]{0,1:T(4,128)}, u32[]{:S(2)}) copy-start(f32[256,4]{0,1:T(4,128)} %param.15) | copy-start | bytes 12292
  7.2 19.2 %copy-start.5 = (s32[256,3]{0,1:T(4,128)S(1)}, s32[256,3]{0,1:T(4,128)}, u32[]{:S(2)}) copy-start(s32[256,3]{0,1:T(4,128)} %param.14) | copy-start | bytes 9220
  7.2 19.7 %copy-start.7 = (s32[256,3]{0,1:T(4,128)S(1)}, s32[256,3]{0,1:T(4,128)}, u32[]{:S(2)}) copy-start(s32[256,3]{0,1:T(4,128)} %param.13) | copy-start | bytes 9220
  7.2 330.4 %reduce-scatter.2.cloned.1.call-start = ((), (), s32[]{:S(2)}) async-start(), calls=%async_computation.1 | async-start | bytes 1572864 | tf_op jit(solution)/shard_map/reduce_scatter | solution.py:118
  9.8 114.3 %collective-permute-start.5 = (bf16[4,1,8,1024]{3,2,1,0:T(8,128)(2,1)}, bf16[4,1,8,1024]{3,2,1,0:T(8,128)(2,1)}, u32[]{:S(2)}, u32[]{:S(2)}) collective-permute-start(bf16[4,1,8,1024]{3,2,1,0:T(8,128)(2,1)} %get-tuple-element.83), channel_id=1, source_target_pairs={{8,0},{16,8},{24,16},{32,24},{40,32},{48,40},{56,48},{9,1},{17,9},... | collective-permute-start | bytes 196616 | tf_op jit(solution)/shard_map/ppermute | solution.py:17
  11.0 114.4 %collective-permute-start.4 = (bf16[4,1,8,1024]{3,2,1,0:T(8,128)(2,1)}, bf16[4,1,8,1024]{3,2,1,0:T(8,128)(2,1)}, u32[]{:S(2)}, u32[]{:S(2)}) collective-permute-start(bf16[4,1,8,1024]{3,2,1,0:T(8,128)(2,1)} %get-tuple-element.82), channel_id=1, source_target_pairs={{0,8},{8,16},{16,24},{24,32},{32,40},{40,48},{48,56},{1,9},{9,17},... | collective-permute-start | bytes 196616 | tf_op jit(solution)/shard_map/ppermute | solution.py:16
  17.0 140.2 %collective-permute-start.1 = (f32[4,1,8,1024]{3,2,1,0:T(8,128)}, f32[4,1,8,1024]{3,2,1,0:T(8,128)S(1)}, u32[]{:S(2)}, u32[]{:S(2)}) collective-permute-start(f32[4,1,8,1024]{3,2,1,0:T(8,128)} %get-tuple-element.66), channel_id=1, source_target_pairs={{0,8},{8,16},{16,24},{24,32},{32,40},{40,48},{48,56},{1,9},{9,17},... | collective-permute-start | bytes 393224 | tf_op jit(solution)/shard_map/ppermute | solution.py:16
  20.6 139.7 %collective-permute-start = (f32[4,1,8,1024]{3,2,1,0:T(8,128)}, f32[4,1,8,1024]{3,2,1,0:T(8,128)}, u32[]{:S(2)}, u32[]{:S(2)}) collective-permute-start(f32[4,1,8,1024]{3,2,1,0:T(8,128)} %get-tuple-element.67), channel_id=1, source_target_pairs={{8,0},{16,8},{24,16},{32,24},{40,32},{48,40},{56,48},{9,1},{17,9},... | collective-permute-start | bytes 393224 | tf_op jit(solution)/shard_map/ppermute | solution.py:17
  22.6 105.3 %collective-permute-start.17 = (bf16[4,1,8,1024]{3,2,1,0:T(8,128)(2,1)}, bf16[4,1,8,1024]{3,2,1,0:T(8,128)(2,1)}, u32[]{:S(2)}, u32[]{:S(2)}) collective-permute-start(bf16[4,1,8,1024]{3,2,1,0:T(8,128)(2,1)} %get-tuple-element.81), channel_id=1, source_target_pairs={{8,0},{16,8},{24,16},{32,24},{40,32},{48,40},{56,48},{9,1},{17,9},... | collective-permute-start | bytes 196616 | tf_op jit(solution)/shard_map/ppermute | solution.py:17
  124.1 7.8 %collective-permute-start.16 = (bf16[4,1,8,1024]{3,2,1,0:T(8,128)(2,1)}, bf16[4,1,8,1024]{3,2,1,0:T(8,128)(2,1)S(1)}, u32[]{:S(2)}, u32[]{:S(2)}) collective-permute-start(bf16[4,1,8,1024]{3,2,1,0:T(8,128)(2,1)} %get-tuple-element.80), channel_id=1, source_target_pairs={{0,8},{8,16},{16,24},{24,32},{32,40},{40,48},{48,56},{1,9},{9,17},... | collective-permute-start | bytes 196616 | tf_op jit(solution)/shard_map/ppermute | solution.py:16
  125.4 8.9 %collective-permute-start.29 = (bf16[4,1,8,1024]{3,2,1,0:T(8,128)(2,1)}, bf16[4,1,8,1024]{3,2,1,0:T(8,128)(2,1)S(1)}, u32[]{:S(2)}, u32[]{:S(2)}) collective-permute-start(bf16[4,1,8,1024]{3,2,1,0:T(8,128)(2,1)} %get-tuple-element.79), channel_id=1, source_target_pairs={{8,0},{16,8},{24,16},{32,24},{40,32},{48,40},{56,48},{9,1},{17,9},... | collective-permute-start | bytes 196616 | tf_op jit(solution)/shard_map/ppermute | solution.py:17
  127.9 10.8 %collective-permute-start.28 = (bf16[4,1,8,1024]{3,2,1,0:T(8,128)(2,1)}, bf16[4,1,8,1024]{3,2,1,0:T(8,128)(2,1)S(1)}, u32[]{:S(2)}, u32[]{:S(2)}) collective-permute-start(bf16[4,1,8,1024]{3,2,1,0:T(8,128)(2,1)} %get-tuple-element.78), channel_id=1, source_target_pairs={{0,8},{8,16},{16,24},{24,32},{32,40},{40,48},{48,56},{1,9},{9,17},... | collective-permute-start | bytes 196616 | tf_op jit(solution)/shard_map/ppermute | solution.py:16
  131.9 20.7 %collective-permute-start.41 = (bf16[4,1,8,1024]{3,2,1,0:T(8,128)(2,1)}, bf16[4,1,8,1024]{3,2,1,0:T(8,128)(2,1)S(1)}, u32[]{:S(2)}, u32[]{:S(2)}) collective-permute-start(bf16[4,1,8,1024]{3,2,1,0:T(8,128)(2,1)} %get-tuple-element.77), channel_id=1, source_target_pairs={{8,0},{16,8},{24,16},{32,24},{40,32},{48,40},{56,48},{9,1},{17,9},... | collective-permute-start | bytes 196616 | tf_op jit(solution)/shard_map/ppermute | solution.py:17
  134.3 20.2 %collective-permute-start.40 = (bf16[4,1,8,1024]{3,2,1,0:T(8,128)(2,1)}, bf16[4,1,8,1024]{3,2,1,0:T(8,128)(2,1)S(1)}, u32[]{:S(2)}, u32[]{:S(2)}) collective-permute-start(bf16[4,1,8,1024]{3,2,1,0:T(8,128)(2,1)} %get-tuple-element.76), channel_id=1, source_target_pairs={{0,8},{8,16},{16,24},{24,32},{32,40},{40,48},{48,56},{1,9},{9,17},... | collective-permute-start | bytes 196616 | tf_op jit(solution)/shard_map/ppermute | solution.py:16
  138.7 24.8 %collective-permute-start.7 = (bf16[4,10,1,1024]{3,2,1,0:T(2,128)(2,1)S(1)}, bf16[4,10,1,1024]{3,2,1,0:T(2,128)(2,1)S(1)}, u32[]{:S(2)}, u32[]{:S(2)}) collective-permute-start(bf16[4,10,1,1024]{3,2,1,0:T(2,128)(2,1)S(1)} %get-tuple-element.75), channel_id=1, source_target_pairs={{1,0},{2,1},{3,2},{4,3},{5,4},{6,5},{7,6},{9,8},{10,9},{11,10},{12... | collective-permute-start | bytes 245768 | tf_op jit(solution)/shard_map/ppermute | solution.py:17
  152.6 14.5 %collective-permute-start.6 = (bf16[4,10,1,1024]{3,2,1,0:T(2,128)(2,1)S(1)}, bf16[4,10,1,1024]{3,2,1,0:T(2,128)(2,1)S(1)}, u32[]{:S(2)}, u32[]{:S(2)}) collective-permute-start(bf16[4,10,1,1024]{3,2,1,0:T(2,128)(2,1)S(1)} %get-tuple-element.74), channel_id=1, source_target_pairs={{0,1},{1,2},{2,3},{3,4},{4,5},{5,6},{6,7},{8,9},{9,10},{10,11},{11... | collective-permute-start | bytes 245768 | tf_op jit(solution)/shard_map/ppermute | solution.py:16
  154.6 25.6 %collective-permute-start.19 = (bf16[4,10,1,1024]{3,2,1,0:T(2,128)(2,1)S(1)}, bf16[4,10,1,1024]{3,2,1,0:T(2,128)(2,1)S(1)}, u32[]{:S(2)}, u32[]{:S(2)}) collective-permute-start(bf16[4,10,1,1024]{3,2,1,0:T(2,128)(2,1)S(1)} %get-tuple-element.73), channel_id=1, source_target_pairs={{1,0},{2,1},{3,2},{4,3},{5,4},{6,5},{7,6},{9,8},{10,9},{11,10},{12... | collective-permute-start | bytes 245768 | tf_op jit(solution)/shard_map/ppermute | solution.py:17
  157.2 27.2 %collective-permute-start.18 = (bf16[4,10,1,1024]{3,2,1,0:T(2,128)(2,1)S(1)}, bf16[4,10,1,1024]{3,2,1,0:T(2,128)(2,1)S(1)}, u32[]{:S(2)}, u32[]{:S(2)}) collective-permute-start(bf16[4,10,1,1024]{3,2,1,0:T(2,128)(2,1)S(1)} %get-tuple-element.72), channel_id=1, source_target_pairs={{0,1},{1,2},{2,3},{3,4},{4,5},{5,6},{6,7},{8,9},{9,10},{10,11},{11... | collective-permute-start | bytes 245768 | tf_op jit(solution)/shard_map/ppermute | solution.py:16
  160.4 51.7 %collective-permute-start.31 = (bf16[4,10,1,1024]{3,2,1,0:T(2,128)(2,1)S(1)}, bf16[4,10,1,1024]{3,2,1,0:T(2,128)(2,1)S(1)}, u32[]{:S(2)}, u32[]{:S(2)}) collective-permute-start(bf16[4,10,1,1024]{3,2,1,0:T(2,128)(2,1)S(1)} %get-tuple-element.71), channel_id=1, source_target_pairs={{1,0},{2,1},{3,2},{4,3},{5,4},{6,5},{7,6},{9,8},{10,9},{11,10},{12... | collective-permute-start | bytes 245768 | tf_op jit(solution)/shard_map/ppermute | solution.py:17
  163.5 8.6 %collective-permute-start.3 = (f32[4,10,1,1024]{3,2,1,0:T(1,128)S(1)}, f32[4,10,1,1024]{3,2,1,0:T(1,128)S(1)}, u32[]{:S(2)}, u32[]{:S(2)}) collective-permute-start(f32[4,10,1,1024]{3,2,1,0:T(1,128)S(1)} %get-tuple-element.47), channel_id=1, source_target_pairs={{0,1},{1,2},{2,3},{3,4},{4,5},{5,6},{6,7},{8,9},{9,10},{10,11},{11... | collective-permute-start | bytes 491528 | tf_op jit(solution)/shard_map/ppermute | solution.py:16
  167.2 8.7 %collective-permute-start.2 = (f32[4,10,1,1024]{3,2,1,0:T(1,128)S(1)}, f32[4,10,1,1024]{3,2,1,0:T(1,128)S(1)}, u32[]{:S(2)}, u32[]{:S(2)}) collective-permute-start(f32[4,10,1,1024]{3,2,1,0:T(1,128)S(1)} %get-tuple-element.46), channel_id=1, source_target_pairs={{1,0},{2,1},{3,2},{4,3},{5,4},{6,5},{7,6},{9,8},{10,9},{11,10},{12... | collective-permute-start | bytes 491528 | tf_op jit(solution)/shard_map/ppermute | solution.py:17
  172.1 7.7 %copy-start.1 = (f32[8,8,1024]{2,1,0:T(8,128)S(1)}, f32[8,8,1024]{2,1,0:T(8,128)}, u32[]{:S(2)}) copy-start(f32[8,8,1024]{2,1,0:T(8,128)} %param.8) | copy-start | bytes 786436
  172.1 7.7 %copy-start.4 = (f32[8,8,1024]{2,1,0:T(8,128)S(1)}, f32[8,8,1024]{2,1,0:T(8,128)}, u32[]{:S(2)}) copy-start(f32[8,8,1024]{2,1,0:T(8,128)} %reshape.127) | copy-start | bytes 786436
  172.1 41.9 %collective-permute-start.30 = (bf16[4,10,1,1024]{3,2,1,0:T(2,128)(2,1)S(1)}, bf16[4,10,1,1024]{3,2,1,0:T(2,128)(2,1)S(1)}, u32[]{:S(2)}, u32[]{:S(2)}) collective-permute-start(bf16[4,10,1,1024]{3,2,1,0:T(2,128)(2,1)S(1)} %get-tuple-element.70), channel_id=1, source_target_pairs={{0,1},{1,2},{2,3},{3,4},{4,5},{5,6},{6,7},{8,9},{9,10},{10,11},{11... | collective-permute-start | bytes 245768 | tf_op jit(solution)/shard_map/ppermute | solution.py:16
  175.9 57.7 %collective-permute-start.43 = (bf16[4,10,1,1024]{3,2,1,0:T(2,128)(2,1)S(1)}, bf16[4,10,1,1024]{3,2,1,0:T(2,128)(2,1)S(1)}, u32[]{:S(2)}, u32[]{:S(2)}) collective-permute-start(bf16[4,10,1,1024]{3,2,1,0:T(2,128)(2,1)S(1)} %get-tuple-element.69), channel_id=1, source_target_pairs={{1,0},{2,1},{3,2},{4,3},{5,4},{6,5},{7,6},{9,8},{10,9},{11,10},{12... | collective-permute-start | bytes 245768 | tf_op jit(solution)/shard_map/ppermute | solution.py:17
  180.1 7.1 %collective-permute-start.9 = (f32[1,8,1024]{2,1,0:T(8,128)S(1)}, f32[1,8,1024]{2,1,0:T(8,128)S(1)}, u32[]{:S(2)}, u32[]{:S(2)}) collective-permute-start(f32[1,8,1024]{2,1,0:T(8,128)S(1)} %get-tuple-element.110), channel_id=1, source_target_pairs={{0,8},{8,16},{16,24},{24,32},{32,40},{40,48},{48,56},{1,9},{9,17},... | collective-permute-start | bytes 98312 | tf_op jit(solution)/shard_map/ppermute | solution.py:16
  184.5 4.7 %collective-permute-start.8 = (f32[1,8,1024]{2,1,0:T(8,128)S(1)}, f32[1,8,1024]{2,1,0:T(8,128)S(1)}, u32[]{:S(2)}, u32[]{:S(2)}) collective-permute-start(f32[1,8,1024]{2,1,0:T(8,128)S(1)} %get-tuple-element.111), channel_id=1, source_target_pairs={{8,0},{16,8},{24,16},{32,24},{40,32},{48,40},{56,48},{9,1},{17,9},... | collective-permute-start | bytes 98312 | tf_op jit(solution)/shard_map/ppermute | solution.py:17
  189.2 7.6 %collective-permute-start.11 = (f32[10,1,1024]{2,1,0:T(1,128)S(1)}, f32[10,1,1024]{2,1,0:T(1,128)S(1)}, u32[]{:S(2)}, u32[]{:S(2)}) collective-permute-start(f32[10,1,1024]{2,1,0:T(1,128)S(1)} %get-tuple-element.99), channel_id=1, source_target_pairs={{0,1},{1,2},{2,3},{3,4},{4,5},{5,6},{6,7},{8,9},{9,10},{10,11},{11... | collective-permute-start | bytes 122888 | tf_op jit(solution)/shard_map/ppermute | solution.py:16
  194.3 5.3 %collective-permute-start.10 = (f32[10,1,1024]{2,1,0:T(1,128)S(1)}, f32[10,1,1024]{2,1,0:T(1,128)S(1)}, u32[]{:S(2)}, u32[]{:S(2)}) collective-permute-start(f32[10,1,1024]{2,1,0:T(1,128)S(1)} %get-tuple-element.98), channel_id=1, source_target_pairs={{1,0},{2,1},{3,2},{4,3},{5,4},{6,5},{7,6},{9,8},{10,9},{11,10},{12... | collective-permute-start | bytes 122888 | tf_op jit(solution)/shard_map/ppermute | solution.py:17
  200.3 4.5 %collective-permute-start.13 = (f32[4,1,8,1024]{3,2,1,0:T(8,128)S(1)}, f32[4,1,8,1024]{3,2,1,0:T(8,128)S(1)}, u32[]{:S(2)}, u32[]{:S(2)}) collective-permute-start(f32[4,1,8,1024]{3,2,1,0:T(8,128)S(1)} %get-tuple-element.61), channel_id=1, source_target_pairs={{0,8},{8,16},{16,24},{24,32},{32,40},{40,48},{48,56},{1,9},{9,17},... | collective-permute-start | bytes 393224 | tf_op jit(solution)/shard_map/ppermute | solution.py:16
  202.9 5.8 %collective-permute-start.12 = (f32[4,1,8,1024]{3,2,1,0:T(8,128)S(1)}, f32[4,1,8,1024]{3,2,1,0:T(8,128)S(1)}, u32[]{:S(2)}, u32[]{:S(2)}) collective-permute-start(f32[4,1,8,1024]{3,2,1,0:T(8,128)S(1)} %get-tuple-element.62), channel_id=1, source_target_pairs={{8,0},{16,8},{24,16},{32,24},{40,32},{48,40},{56,48},{9,1},{17,9},... | collective-permute-start | bytes 393224 | tf_op jit(solution)/shard_map/ppermute | solution.py:17
  204.8 28.8 %collective-permute-start.42 = (bf16[4,10,1,1024]{3,2,1,0:T(2,128)(2,1)S(1)}, bf16[4,10,1,1024]{3,2,1,0:T(2,128)(2,1)S(1)}, u32[]{:S(2)}, u32[]{:S(2)}) collective-permute-start(bf16[4,10,1,1024]{3,2,1,0:T(2,128)(2,1)S(1)} %get-tuple-element.68), channel_id=1, source_target_pairs={{0,1},{1,2},{2,3},{3,4},{4,5},{5,6},{6,7},{8,9},{9,10},{10,11},{11... | collective-permute-start | bytes 245768 | tf_op jit(solution)/shard_map/ppermute | solution.py:16
  208.8 5.9 %collective-permute-start.15 = (f32[4,10,1,1024]{3,2,1,0:T(1,128)S(1)}, f32[4,10,1,1024]{3,2,1,0:T(1,128)S(1)}, u32[]{:S(2)}, u32[]{:S(2)}) collective-permute-start(f32[4,10,1,1024]{3,2,1,0:T(1,128)S(1)} %get-tuple-element.43), channel_id=1, source_target_pairs={{0,1},{1,2},{2,3},{3,4},{4,5},{5,6},{6,7},{8,9},{9,10},{10,11},{11... | collective-permute-start | bytes 491528 | tf_op jit(solution)/shard_map/ppermute | solution.py:16
  212.1 6.6 %collective-permute-start.14 = (f32[4,10,1,1024]{3,2,1,0:T(1,128)S(1)}, f32[4,10,1,1024]{3,2,1,0:T(1,128)S(1)}, u32[]{:S(2)}, u32[]{:S(2)}) collective-permute-start(f32[4,10,1,1024]{3,2,1,0:T(1,128)S(1)} %get-tuple-element.42), channel_id=1, source_target_pairs={{1,0},{2,1},{3,2},{4,3},{5,4},{6,5},{7,6},{9,8},{10,9},{11,10},{12... | collective-permute-start | bytes 491528 | tf_op jit(solution)/shard_map/ppermute | solution.py:17
  214.7 5.1 %copy-start.3 = (f32[8,8,1024]{2,1,0:T(8,128)S(1)}, f32[8,8,1024]{2,1,0:T(8,128)}, u32[]{:S(2)}) copy-start(f32[8,8,1024]{2,1,0:T(8,128)} %reshape.128) | copy-start | bytes 786436
  220.2 5.5 %collective-permute-start.21 = (f32[1,8,1024]{2,1,0:T(8,128)S(1)}, f32[1,8,1024]{2,1,0:T(8,128)S(1)}, u32[]{:S(2)}, u32[]{:S(2)}) collective-permute-start(f32[1,8,1024]{2,1,0:T(8,128)S(1)} %get-tuple-element.107), channel_id=1, source_target_pairs={{0,8},{8,16},{16,24},{24,32},{32,40},{40,48},{48,56},{1,9},{9,17},... | collective-permute-start | bytes 98312 | tf_op jit(solution)/shard_map/ppermute | solution.py:16
  223.8 4.7 %collective-permute-start.20 = (f32[1,8,1024]{2,1,0:T(8,128)S(1)}, f32[1,8,1024]{2,1,0:T(8,128)S(1)}, u32[]{:S(2)}, u32[]{:S(2)}) collective-permute-start(f32[1,8,1024]{2,1,0:T(8,128)S(1)} %get-tuple-element.108), channel_id=1, source_target_pairs={{8,0},{16,8},{24,16},{32,24},{40,32},{48,40},{56,48},{9,1},{17,9},... | collective-permute-start | bytes 98312 | tf_op jit(solution)/shard_map/ppermute | solution.py:17
  228.5 5.8 %collective-permute-start.23 = (f32[10,1,1024]{2,1,0:T(1,128)S(1)}, f32[10,1,1024]{2,1,0:T(1,128)S(1)}, u32[]{:S(2)}, u32[]{:S(2)}) collective-permute-start(f32[10,1,1024]{2,1,0:T(1,128)S(1)} %get-tuple-element.95), channel_id=1, source_target_pairs={{0,1},{1,2},{2,3},{3,4},{4,5},{5,6},{6,7},{8,9},{9,10},{10,11},{11... | collective-permute-start | bytes 122888 | tf_op jit(solution)/shard_map/ppermute | solution.py:16
  231.7 5.3 %collective-permute-start.22 = (f32[10,1,1024]{2,1,0:T(1,128)S(1)}, f32[10,1,1024]{2,1,0:T(1,128)S(1)}, u32[]{:S(2)}, u32[]{:S(2)}) collective-permute-start(f32[10,1,1024]{2,1,0:T(1,128)S(1)} %get-tuple-element.94), channel_id=1, source_target_pairs={{1,0},{2,1},{3,2},{4,3},{5,4},{6,5},{7,6},{9,8},{10,9},{11,10},{12... | collective-permute-start | bytes 122888 | tf_op jit(solution)/shard_map/ppermute | solution.py:17
  237.7 6.2 %collective-permute-start.25 = (f32[4,1,8,1024]{3,2,1,0:T(8,128)S(1)}, f32[4,1,8,1024]{3,2,1,0:T(8,128)S(1)}, u32[]{:S(2)}, u32[]{:S(2)}) collective-permute-start(f32[4,1,8,1024]{3,2,1,0:T(8,128)S(1)} %get-tuple-element.56), channel_id=1, source_target_pairs={{0,8},{8,16},{16,24},{24,32},{32,40},{40,48},{48,56},{1,9},{9,17},... | collective-permute-start | bytes 393224 | tf_op jit(solution)/shard_map/ppermute | solution.py:16
  242.0 6.2 %collective-permute-start.24 = (f32[4,1,8,1024]{3,2,1,0:T(8,128)S(1)}, f32[4,1,8,1024]{3,2,1,0:T(8,128)S(1)}, u32[]{:S(2)}, u32[]{:S(2)}) collective-permute-start(f32[4,1,8,1024]{3,2,1,0:T(8,128)S(1)} %get-tuple-element.57), channel_id=1, source_target_pairs={{8,0},{16,8},{24,16},{32,24},{40,32},{48,40},{56,48},{9,1},{17,9},... | collective-permute-start | bytes 393224 | tf_op jit(solution)/shard_map/ppermute | solution.py:17
  248.5 6.4 %collective-permute-start.27 = (f32[4,10,1,1024]{3,2,1,0:T(1,128)S(1)}, f32[4,10,1,1024]{3,2,1,0:T(1,128)S(1)}, u32[]{:S(2)}, u32[]{:S(2)}) collective-permute-start(f32[4,10,1,1024]{3,2,1,0:T(1,128)S(1)} %get-tuple-element.39), channel_id=1, source_target_pairs={{0,1},{1,2},{2,3},{3,4},{4,5},{5,6},{6,7},{8,9},{9,10},{10,11},{11... | collective-permute-start | bytes 491528 | tf_op jit(solution)/shard_map/ppermute | solution.py:16
  251.5 6.6 %collective-permute-start.26 = (f32[4,10,1,1024]{3,2,1,0:T(1,128)S(1)}, f32[4,10,1,1024]{3,2,1,0:T(1,128)S(1)}, u32[]{:S(2)}, u32[]{:S(2)}) collective-permute-start(f32[4,10,1,1024]{3,2,1,0:T(1,128)S(1)} %get-tuple-element.38), channel_id=1, source_target_pairs={{1,0},{2,1},{3,2},{4,3},{5,4},{6,5},{7,6},{9,8},{10,9},{11,10},{12... | collective-permute-start | bytes 491528 | tf_op jit(solution)/shard_map/ppermute | solution.py:17
  254.9 4.4 %copy-start.2 = (f32[8,8,1024]{2,1,0:T(8,128)S(1)}, f32[8,8,1024]{2,1,0:T(8,128)}, u32[]{:S(2)}) copy-start(f32[8,8,1024]{2,1,0:T(8,128)} %reshape.129) | copy-start | bytes 786436
  259.6 5.5 %collective-permute-start.33 = (f32[1,8,1024]{2,1,0:T(8,128)S(1)}, f32[1,8,1024]{2,1,0:T(8,128)S(1)}, u32[]{:S(2)}, u32[]{:S(2)}) collective-permute-start(f32[1,8,1024]{2,1,0:T(8,128)S(1)} %get-tuple-element.104), channel_id=1, source_target_pairs={{0,8},{8,16},{16,24},{24,32},{32,40},{40,48},{48,56},{1,9},{9,17},... | collective-permute-start | bytes 98312 | tf_op jit(solution)/shard_map/ppermute | solution.py:16
  263.6 4.7 %collective-permute-start.32 = (f32[1,8,1024]{2,1,0:T(8,128)S(1)}, f32[1,8,1024]{2,1,0:T(8,128)S(1)}, u32[]{:S(2)}, u32[]{:S(2)}) collective-permute-start(f32[1,8,1024]{2,1,0:T(8,128)S(1)} %get-tuple-element.105), channel_id=1, source_target_pairs={{8,0},{16,8},{24,16},{32,24},{40,32},{48,40},{56,48},{9,1},{17,9},... | collective-permute-start | bytes 98312 | tf_op jit(solution)/shard_map/ppermute | solution.py:17
  268.3 5.3 %collective-permute-start.35 = (f32[10,1,1024]{2,1,0:T(1,128)S(1)}, f32[10,1,1024]{2,1,0:T(1,128)S(1)}, u32[]{:S(2)}, u32[]{:S(2)}) collective-permute-start(f32[10,1,1024]{2,1,0:T(1,128)S(1)} %get-tuple-element.91), channel_id=1, source_target_pairs={{0,1},{1,2},{2,3},{3,4},{4,5},{5,6},{6,7},{8,9},{9,10},{10,11},{11... | collective-permute-start | bytes 122888 | tf_op jit(solution)/shard_map/ppermute | solution.py:16
  271.5 5.3 %collective-permute-start.34 = (f32[10,1,1024]{2,1,0:T(1,128)S(1)}, f32[10,1,1024]{2,1,0:T(1,128)S(1)}, u32[]{:S(2)}, u32[]{:S(2)}) collective-permute-start(f32[10,1,1024]{2,1,0:T(1,128)S(1)} %get-tuple-element.90), channel_id=1, source_target_pairs={{1,0},{2,1},{3,2},{4,3},{5,4},{6,5},{7,6},{9,8},{10,9},{11,10},{12... | collective-permute-start | bytes 122888 | tf_op jit(solution)/shard_map/ppermute | solution.py:17
  277.5 5.4 %collective-permute-start.37 = (f32[4,1,8,1024]{3,2,1,0:T(8,128)S(1)}, f32[4,1,8,1024]{3,2,1,0:T(8,128)S(1)}, u32[]{:S(2)}, u32[]{:S(2)}) collective-permute-start(f32[4,1,8,1024]{3,2,1,0:T(8,128)S(1)} %get-tuple-element.51), channel_id=1, source_target_pairs={{0,8},{8,16},{16,24},{24,32},{32,40},{40,48},{48,56},{1,9},{9,17},... | collective-permute-start | bytes 393224 | tf_op jit(solution)/shard_map/ppermute | solution.py:16
  281.0 5.7 %collective-permute-start.36 = (f32[4,1,8,1024]{3,2,1,0:T(8,128)S(1)}, f32[4,1,8,1024]{3,2,1,0:T(8,128)S(1)}, u32[]{:S(2)}, u32[]{:S(2)}) collective-permute-start(f32[4,1,8,1024]{3,2,1,0:T(8,128)S(1)} %get-tuple-element.52), channel_id=1, source_target_pairs={{8,0},{16,8},{24,16},{32,24},{40,32},{48,40},{56,48},{9,1},{17,9},... | collective-permute-start | bytes 393224 | tf_op jit(solution)/shard_map/ppermute | solution.py:17
  286.9 6.0 %collective-permute-start.39 = (f32[4,10,1,1024]{3,2,1,0:T(1,128)S(1)}, f32[4,10,1,1024]{3,2,1,0:T(1,128)S(1)}, u32[]{:S(2)}, u32[]{:S(2)}) collective-permute-start(f32[4,10,1,1024]{3,2,1,0:T(1,128)S(1)} %get-tuple-element.35), channel_id=1, source_target_pairs={{0,1},{1,2},{2,3},{3,4},{4,5},{5,6},{6,7},{8,9},{9,10},{10,11},{11... | collective-permute-start | bytes 491528 | tf_op jit(solution)/shard_map/ppermute | solution.py:16
  290.7 6.6 %collective-permute-start.38 = (f32[4,10,1,1024]{3,2,1,0:T(1,128)S(1)}, f32[4,10,1,1024]{3,2,1,0:T(1,128)S(1)}, u32[]{:S(2)}, u32[]{:S(2)}) collective-permute-start(f32[4,10,1,1024]{3,2,1,0:T(1,128)S(1)} %get-tuple-element.34), channel_id=1, source_target_pairs={{1,0},{2,1},{3,2},{4,3},{5,4},{6,5},{7,6},{9,8},{10,9},{11,10},{12... | collective-permute-start | bytes 491528 | tf_op jit(solution)/shard_map/ppermute | solution.py:17
  298.8 4.5 %collective-permute-start.45 = (f32[1,8,1024]{2,1,0:T(8,128)S(1)}, f32[1,8,1024]{2,1,0:T(8,128)S(1)}, u32[]{:S(2)}, u32[]{:S(2)}) collective-permute-start(f32[1,8,1024]{2,1,0:T(8,128)S(1)} %get-tuple-element.101), channel_id=1, source_target_pairs={{0,8},{8,16},{16,24},{24,32},{32,40},{40,48},{48,56},{1,9},{9,17},... | collective-permute-start | bytes 98312 | tf_op jit(solution)/shard_map/ppermute | solution.py:16
  301.6 4.7 %collective-permute-start.44 = (f32[1,8,1024]{2,1,0:T(8,128)S(1)}, f32[1,8,1024]{2,1,0:T(8,128)S(1)}, u32[]{:S(2)}, u32[]{:S(2)}) collective-permute-start(f32[1,8,1024]{2,1,0:T(8,128)S(1)} %get-tuple-element.102), channel_id=1, source_target_pairs={{8,0},{16,8},{24,16},{32,24},{40,32},{48,40},{56,48},{9,1},{17,9},... | collective-permute-start | bytes 98312 | tf_op jit(solution)/shard_map/ppermute | solution.py:17
  306.3 5.3 %collective-permute-start.47 = (f32[10,1,1024]{2,1,0:T(1,128)S(1)}, f32[10,1,1024]{2,1,0:T(1,128)S(1)}, u32[]{:S(2)}, u32[]{:S(2)}) collective-permute-start(f32[10,1,1024]{2,1,0:T(1,128)S(1)} %get-tuple-element.87), channel_id=1, source_target_pairs={{0,1},{1,2},{2,3},{3,4},{4,5},{5,6},{6,7},{8,9},{9,10},{10,11},{11... | collective-permute-start | bytes 122888 | tf_op jit(solution)/shard_map/ppermute | solution.py:16
  309.5 5.3 %collective-permute-start.46 = (f32[10,1,1024]{2,1,0:T(1,128)S(1)}, f32[10,1,1024]{2,1,0:T(1,128)S(1)}, u32[]{:S(2)}, u32[]{:S(2)}) collective-permute-start(f32[10,1,1024]{2,1,0:T(1,128)S(1)} %get-tuple-element.86), channel_id=1, source_target_pairs={{1,0},{2,1},{3,2},{4,3},{5,4},{6,5},{7,6},{9,8},{10,9},{11,10},{12... | collective-permute-start | bytes 122888 | tf_op jit(solution)/shard_map/ppermute | solution.py:17
Sparse Core Ops, SparseCore 0:
  317.7 19.9 reduce-scatter.1
